TPU v7x, 128 devices: a whole 4x4x4 slice. The times are simulated.
128 devices in a mesh: fsdp: 2 (over core), ctx: 64 (over z, x, y).
Axes of the slice: x: 4, y: 4, z: 4, core: 2. Of those that a mesh axis runs over, the one named last changes fastest.
Arguments:
- token_ids: int32 [2, 8192], P('fsdp', 'ctx'), may hold values from 0 to 511
- embedding: bfloat16 [512, 4096], P(None, 'fsdp'), may hold values from -5 to 5
- conv_taps: float32 [3, 3, 4096], replicated, may hold values from -2.5 to 2.5
- residues: float32 [4096, 16], replicated, may hold values from -1.2 to 1.2
- decays: float32 [4096, 16], replicated, may hold values from 2.4414062e-06 to 0.05
- filter_seed: int32 [4096, 16], replicated, may hold values from 0 to 4095
- skip_gain: float32 [4096], replicated, may hold values from 0.5 to 1.5
- cotangent: float32 [2, 4096, 8192], P('fsdp', None, 'ctx'), may hold values from -6 to 6
Outputs:
- mixer_out: float32 [2, 4096, 8192], P('fsdp', None, 'ctx')
- embed_grad: float32 [512, 4096], P(None, 'fsdp')
All inputs are finite; a program needn't handle non-finite values.
Results may differ from a plain program's by a relative error of at most 0.0006.
Values may be sent and summed in bfloat16 or wider, within the bound.
A program may use at most 320 MiB of HBM per device.

v0:
```python
import math
import jax
import jax.numpy as jnp
from jax import lax
from jax.sharding import PartitionSpec as P

PERIOD = 4096
HIGHEST = lax.Precision.HIGHEST
TWO_PI = 2.0 * math.pi


def from_behind(value, axis, steps):
    count = lax.axis_size(axis)
    leading, last = (max(0, -steps), min(count, count - steps))
    return lax.ppermute(value, axis, [(source, source + steps) for source in range(leading, last)])


def dft_tables(half_blocks, tok_block):
    full_blocks = 2 * half_blocks
    total_len = full_blocks * tok_block
    outer = (
        jnp.arange(half_blocks, dtype=jnp.int32)[:, None]
        * jnp.arange(full_blocks, dtype=jnp.int32)[None, :]
        % full_blocks
    )
    outer_angle = TWO_PI / full_blocks * outer.astype(jnp.float32)
    twist = (
        jnp.arange(full_blocks, dtype=jnp.int32)[:, None]
        * jnp.arange(tok_block, dtype=jnp.int32)[None, :]
        % total_len
    )
    twist_angle = TWO_PI / total_len * twist.astype(jnp.float32)
    inner = (
        jnp.arange(tok_block, dtype=jnp.int32)[:, None]
        * jnp.arange(tok_block, dtype=jnp.int32)[None, :]
        % tok_block
    )
    inner_angle = TWO_PI / tok_block * inner.astype(jnp.float32)
    return (
        jnp.cos(outer_angle),
        jnp.sin(outer_angle),
        jnp.cos(twist_angle),
        jnp.sin(twist_angle),
        jnp.cos(inner_angle),
        jnp.sin(inner_angle),
    )


def forward_dft(blocks, tables):
    outer_cos, outer_sin, twist_cos, twist_sin, inner_cos, inner_sin = tables
    part_real = jnp.einsum("bcst,sk->bckt", blocks, outer_cos, precision=HIGHEST)
    part_imag = -jnp.einsum("bcst,sk->bckt", blocks, outer_sin, precision=HIGHEST)
    turned_real = part_real * twist_cos + part_imag * twist_sin
    turned_imag = part_imag * twist_cos - part_real * twist_sin
    spec_real = jnp.einsum("bckt,tm->bckm", turned_real, inner_cos, precision=HIGHEST) + jnp.einsum(
        "bckt,tm->bckm", turned_imag, inner_sin, precision=HIGHEST
    )
    spec_imag = jnp.einsum("bckt,tm->bckm", turned_imag, inner_cos, precision=HIGHEST) - jnp.einsum(
        "bckt,tm->bckm", turned_real, inner_sin, precision=HIGHEST
    )
    return (spec_real, spec_imag)


def inverse_dft(prod_real, prod_imag, tables):
    outer_cos, outer_sin, twist_cos, twist_sin, inner_cos, inner_sin = tables
    total_len = outer_cos.shape[1] * inner_cos.shape[0]
    back_real = jnp.einsum("bckm,tm->bckt", prod_real, inner_cos, precision=HIGHEST) - jnp.einsum(
        "bckm,tm->bckt", prod_imag, inner_sin, precision=HIGHEST
    )
    back_imag = jnp.einsum("bckm,tm->bckt", prod_imag, inner_cos, precision=HIGHEST) + jnp.einsum(
        "bckm,tm->bckt", prod_real, inner_sin, precision=HIGHEST
    )
    turned_real = back_real * twist_cos - back_imag * twist_sin
    turned_imag = back_imag * twist_cos + back_real * twist_sin
    signal = jnp.einsum("bckt,sk->bcst", turned_real, outer_cos, precision=HIGHEST) - jnp.einsum(
        "bckt,sk->bcst", turned_imag, outer_sin, precision=HIGHEST
    )
    return signal / total_len


def apply_filter(spread, kernel_real, kernel_imag, tables, adjoint_sign):
    batch_rows = spread.shape[0]
    slab_size = spread.shape[1]
    half_blocks = tables[0].shape[0]
    tok_block = tables[4].shape[0]
    spec_real, spec_imag = forward_dft(
        spread.reshape(batch_rows, slab_size, half_blocks, tok_block), tables
    )
    prod_real = kernel_real * spec_real - adjoint_sign * kernel_imag * spec_imag
    prod_imag = kernel_real * spec_imag + adjoint_sign * kernel_imag * spec_real
    return inverse_dft(prod_real, prod_imag, tables).reshape(spread.shape)


def body(token_ids, embedding, conv_taps, residues, decays, filter_seed, skip_gain, cotangent):
    ctx_size = lax.axis_size("ctx")
    ctx_rank = lax.axis_index("ctx")
    model_width = conv_taps.shape[2]
    vocab_size = embedding.shape[0]
    tok_block = token_ids.shape[1]
    full_table = lax.all_gather(embedding, "fsdp", axis=1, tiled=True)
    gain_local = skip_gain[:, None]
    signal = jnp.swapaxes(jnp.take(full_table, token_ids, axis=0), 1, 2)
    before = from_behind(signal[:, :, tok_block - 2 :], "ctx", 1)
    extended = jnp.concatenate([before, signal], axis=2).astype(jnp.float32)

    def causal_mix(tap_set):
        return (
            tap_set[0][:, None] * extended[:, :, 2:]
            + tap_set[1][:, None] * extended[:, :, 1 : tok_block + 1]
            + tap_set[2][:, None] * extended[:, :, :tok_block]
        )

    query_stream = causal_mix(conv_taps[0])
    key_stream = causal_mix(conv_taps[1])
    value_stream = causal_mix(conv_taps[2])
    mixed_in = key_stream * value_stream
    grad_long = cotangent * query_stream
    seq_len = tok_block * ctx_size
    slab_size = model_width // ctx_size
    slab_start = ctx_rank * slab_size
    positions = jnp.arange(seq_len, dtype=jnp.int32)
    decay_rate = lax.dynamic_slice_in_dim(decays, slab_start, slab_size, 0)[:, :, None]
    seed_part = lax.dynamic_slice_in_dim(filter_seed, slab_start, slab_size, 0)[:, :, None]
    residue_part = lax.dynamic_slice_in_dim(residues, slab_start, slab_size, 0)[:, :, None]
    phase_int = seed_part * positions[None, None, :] % PERIOD
    weight = residue_part * jnp.sqrt(decay_rate + 1.0 / seq_len)
    kernel = jnp.sum(
        weight
        * jnp.exp(-decay_rate * positions.astype(jnp.float32)[None, None, :])
        * jnp.cos(TWO_PI / PERIOD * phase_int.astype(jnp.float32)),
        axis=1,
    )
    tables = dft_tables(ctx_size, tok_block)
    kernel_real, kernel_imag = forward_dft(
        kernel.reshape(1, slab_size, ctx_size, tok_block), tables
    )
    spread_mix, spread_grad = (
        lax.all_to_all(mixed_in, "ctx", split_axis=1, concat_axis=2, tiled=True),
        lax.all_to_all(grad_long, "ctx", split_axis=1, concat_axis=2, tiled=True),
    )
    conv_part = apply_filter(spread_mix, kernel_real, kernel_imag, tables, 1.0)
    corr_part = apply_filter(spread_grad, kernel_real, kernel_imag, tables, -1.0)
    conv_out, correlated = (
        lax.all_to_all(conv_part, "ctx", split_axis=2, concat_axis=1, tiled=True),
        lax.all_to_all(corr_part, "ctx", split_axis=2, concat_axis=1, tiled=True),
    )
    long_out = conv_out + gain_local * mixed_in
    mixer_local = query_stream * long_out
    grad_query = cotangent * long_out
    grad_mixed = correlated + gain_local * grad_long
    grad_key = grad_mixed * value_stream
    grad_value = grad_mixed * key_stream

    def tap_term(tap_index):
        return (
            conv_taps[0][tap_index][:, None] * grad_query
            + conv_taps[1][tap_index][:, None] * grad_key
            + conv_taps[2][tap_index][:, None] * grad_value
        )

    first_term = tap_term(0)
    second_term = tap_term(1)
    third_term = tap_term(2)
    next_rows = from_behind(jnp.stack([second_term[:, :, :2], third_term[:, :, :2]]), "ctx", -1)
    grad_signal = (
        first_term
        + jnp.concatenate([second_term, next_rows[0]], axis=2)[:, :, 1 : tok_block + 1]
        + jnp.concatenate([third_term, next_rows[1]], axis=2)[:, :, 2 : tok_block + 2]
    )
    one_hot = (
        token_ids[:, :, None] == jnp.arange(vocab_size, dtype=jnp.int32)[None, None, :]
    ).astype(jnp.float32)
    partial_grad = jnp.einsum("btv,bct->vc", one_hot, grad_signal, precision=HIGHEST)
    half_grad = lax.psum_scatter(partial_grad, "fsdp", scatter_dimension=1, tiled=True)
    embed_grad = lax.psum(half_grad, "ctx")
    return (mixer_local, embed_grad)


def solution(mesh):
    placed = (P("fsdp", "ctx"), P(None, "fsdp"), P(), P(), P(), P(), P(), P("fsdp", None, "ctx"))
    return jax.shard_map(
        body,
        mesh=mesh,
        in_specs=placed,
        out_specs=(P("fsdp", None, "ctx"), P(None, "fsdp")),
        check_vma=False,
    )
```

profile of v0, /device:TPU:0, one launch (start us, length us, event | category | flops | bytes accessed | tf_op | source)
XLA Modules:
  0.0 764.9 jit_solution(1966881312093857230)
XLA Ops:
  12.0 16.5 %all-gather.2.cloned.1.call-done = bf16[512,4096]{1,0:T(8,128)(2,1)} async-done(((bf16[512,2048]{1,0:T(8,128)(2,1)}), bf16[512,4096]{1,0:T(8,128)(2,1)}) %all-gather.2.cloned.1.call-update) | async-done | bytes 4194320 | tf_op jit(solution)/shard_map/all_gather | solution.py:100
  52.2 10.4 %all-to-all-start.2 = ((f32[1,4096,128]{2,0,1:T(1,128)}), f32[1,4096,128]{2,0,1:T(1,128)S(1)}, u32[]{:S(2)}, u32[]{:S(2)}) async-start(f32[1,4096,128]{2,0,1:T(1,128)} %copy.93), calls=%async_computation.2 | async-start | bytes 4194304 | tf_op jit(solution)/shard_map/all_to_all | solution.py:139
  62.6 133.4 %fusion.5 = f32[64,8192]{1,0:T(8,128)S(1)} fusion(s32[64,16]{1,0:T(8,128)S(1)} %copy.84, f32[8192]{0:T(1024)S(1)} %copy-done.32, f32[64,16]{1,0:T(8,128)S(1)} %copy.83, f32[64,16]{1,0:T(8,128)S(1)} %copy.82), kind=kLoop, calls=%fused_computation.9 | loop fusion | flops 150470656 | bytes 2142208 | tf_op jit(solution)/shard_map/reduce_sum | solution.py:127
  221.2 10.9 %all-to-all-start = ((f32[1,4096,128]{2,0,1:T(1,128)}), f32[1,4096,128]{2,0,1:T(1,128)}, u32[]{:S(2)}, u32[]{:S(2)}) async-start(f32[1,4096,128]{2,0,1:T(1,128)} %copy.85), calls=%async_computation | async-start | bytes 4194304 | tf_op jit(solution)/shard_map/all_to_all | solution.py:138
  232.2 8.8 %fusion.58 = f32[64,128,128]{2,1,0:T(8,128)} fusion(f32[64,128,128]{2,1,0:T(8,128)} %fusion.27, f32[128,64,128]{2,0,1:T(8,128)} %copy-done.6, f32[128,64,128]{2,0,1:T(8,128)} %copy-done.4, f32[128,128]{1,0:T(8,128)S(1)} %get-tuple-element.45, f32[128,128]{1,0:T(8,128)S(1)} %get-tuple-element.46), kind=kOutput, calls=%fused_computation.76 | convolution fusion | flops 1616084992 | bytes 16908288 | tf_op jit(solution)/shard_map/bckt,tm->bckm/dot_general | solution.py:58
  247.7 7.0 fusion.81
  254.7 7.3 fusion.83
  310.8 19.4 %multiply_add_fusion = (f32[64,128,128]{2,1,0:T(8,128)}, f32[64,128,128]{2,1,0:T(8,128)}, f32[64,128,128]{2,1,0:T(8,128)}, f32[64,128,128]{2,1,0:T(8,128)}) fusion(f32[64,128,128]{2,1,0:T(8,128)} %fusion.55, f32[64,128,128]{2,1,0:T(8,128)} %fusion.70, f32[64,128,128]{2,1,0:T(8,128)} %fusion.58, f32[64,128,128]{2,1,0:T(8,128)} %fusion.64, ...), kind=kOutput, calls=%fused_computation.63 | convolution fusion | flops 1629716480 | bytes 50462720 | tf_op jit(solution)/shard_map/bckt,tm->bckm/dot_general | solution.py:55
  330.1 6.5 fusion.147
  357.7 38.4 %reduce.2 = f32[8192,64]{1,0:T(8,128)} reduce(f32[8192,1,64]{2,1,0:T(1,128)} %bitcast.330, f32[]{:T(128)} %broadcast.309), dimensions={1}, to_apply=%bitcast.304.reduce_sub_computation | reduce | bytes 4194308
  401.6 10.7 %all-to-all-start.3 = ((f32[64,1,8192]{2,1,0:T(1,128)}), f32[64,1,8192]{2,1,0:T(1,128)}, u32[]{:S(2)}, u32[]{:S(2)}) async-start(f32[64,1,8192]{2,1,0:T(1,128)} %reshape.405), calls=%async_computation.3 | async-start | bytes 4194304 | tf_op jit(solution)/shard_map/all_to_all | solution.py:145
  412.3 6.4 fusion.155
  439.2 38.4 %reduce = f32[8192,64]{1,0:T(8,128)} reduce(f32[8192,1,64]{2,1,0:T(1,128)} %bitcast.331, f32[]{:T(128)} %broadcast.309), dimensions={1}, to_apply=%bitcast.302.reduce_sub_computation | reduce | bytes 4194308
  483.1 10.5 %all-to-all-start.1 = ((f32[64,1,8192]{2,1,0:T(1,128)}), f32[64,1,8192]{2,1,0:T(1,128)}, u32[]{:S(2)}, u32[]{:S(2)}) async-start(f32[64,1,8192]{2,1,0:T(1,128)} %reshape.403), calls=%async_computation.1 | async-start | bytes 4194304 | tf_op jit(solution)/shard_map/all_to_all | solution.py:144
  494.0 7.5 reduce.3
  501.6 6.6 reshape.406
  508.1 9.1 %copy.96 = f32[1,64,8192]{2,0,1:T(1,128)S(1)} copy(f32[1,64,8192]{1,0,2:T(1,128)} %bitcast.328) | data formatting | bytes 4194304 | tf_op jit(solution)/shard_map/all_to_all | solution.py:145
  522.7 7.5 reduce.1
  530.2 6.8 reshape.404
  536.9 10.5 %copy.88 = f32[1,64,8192]{2,0,1:T(1,128)} copy(f32[1,64,8192]{1,0,2:T(1,128)} %bitcast.329) | data formatting | bytes 4194304 | tf_op jit(solution)/shard_map/all_to_all | solution.py:144
  554.7 10.9 %multiply_add_fusion.3 = (f32[1,4096,128]{1,2,0:T(8,128)}, f32[1,4096,128]{1,2,0:T(8,128)}, f32[1,4096,128]{1,2,0:T(8,128)}, f32[1,4096,128]{1,2,0:T(8,128)}, f32[1,4096,128]{1,2,0:T(8,128)}) fusion(f32[4096]{0:T(1024)S(1)} %bitcast.354, f32[4096]{0:T(1024)S(1)} %bitcast.350, f32[4096]{0:T(1024)S(1)} %bitcast.352, f32[1,4096,128]{1,2,0:T(8,128)S(1)} %copy-done.13, ...), kind=kLoop, calls=%fused_computation.102 | loop fusion | flops 6815744 | bytes 27328512 | tf_op jit(solution)/shard_map/add | solution.py:156
  576.5 6.5 fusion.75
  583.0 24.6 %reduce-scatter.2.cloned.1.call-done = f32[512,2048]{1,0:T(8,128)} async-done(((f32[512,4096]{1,0:T(8,128)}), f32[512,2048]{1,0:T(8,128)}) %reduce-scatter.2.cloned.1.call-update) | async-done | bytes 4194320 | tf_op jit(solution)/shard_map/reduce_scatter | solution.py:174
  609.5 144.1 %all-reduce.2.cloned.1.call-done = f32[512,2048]{1,0:T(8,128)} async-done(((f32[512,2048]{1,0:T(8,128)}), f32[512,2048]{1,0:T(8,128)}) %all-reduce.2.cloned.1.call-update) | async-done | bytes 4194320 | tf_op jit(solution)/shard_map/psum | solution.py:175
  (144 shorter events, 191.7 us)
Async XLA Ops:
  7.2 31.2 %copy-start = (s32[4096,16]{0,1:T(8,128)S(1)}, s32[4096,16]{0,1:T(8,128)}, u32[]{:S(2)}) copy-start(s32[4096,16]{0,1:T(8,128)} %param.13) | copy-start | bytes 786436
  7.2 21.3 %all-gather.2.cloned.1.call-start = ((), (), s32[]{:S(2)}) async-start(), calls=%async_computation.5 | async-start | bytes 6291456 | tf_op jit(solution)/shard_map/all_gather | solution.py:100
  11.9 29.8 %copy-start.20 = (f32[1,1,4096]{2,1,0:T(1,128)}, f32[1,1,4096]{2,1,0:T(1,128)S(1)}, u32[]{:S(2)}) copy-start(f32[1,1,4096]{2,1,0:T(1,128)S(1)} %get-tuple-element.36) | copy-start | bytes 49156
  11.9 29.8 %copy-start.22 = (f32[1,1,4096]{2,1,0:T(1,128)}, f32[1,1,4096]{2,1,0:T(1,128)S(1)}, u32[]{:S(2)}) copy-start(f32[1,1,4096]{2,1,0:T(1,128)S(1)} %get-tuple-element.38) | copy-start | bytes 49156
  11.9 29.8 %copy-start.24 = (f32[1,1,4096]{2,1,0:T(1,128)}, f32[1,1,4096]{2,1,0:T(1,128)S(1)}, u32[]{:S(2)}) copy-start(f32[1,1,4096]{2,1,0:T(1,128)S(1)} %get-tuple-element.41) | copy-start | bytes 49156
  11.9 29.8 %copy-start.26 = (f32[1,1,4096]{2,1,0:T(1,128)}, f32[1,1,4096]{2,1,0:T(1,128)S(1)}, u32[]{:S(2)}) copy-start(f32[1,1,4096]{2,1,0:T(1,128)S(1)} %get-tuple-element.34) | copy-start | bytes 49156
  11.9 29.8 %copy-start.28 = (f32[1,1,4096]{2,1,0:T(1,128)}, f32[1,1,4096]{2,1,0:T(1,128)S(1)}, u32[]{:S(2)}) copy-start(f32[1,1,4096]{2,1,0:T(1,128)S(1)} %get-tuple-element.35) | copy-start | bytes 49156
  12.0 29.8 %copy-start.30 = (f32[1,1,4096]{2,1,0:T(1,128)}, f32[1,1,4096]{2,1,0:T(1,128)S(1)}, u32[]{:S(2)}) copy-start(f32[1,1,4096]{2,1,0:T(1,128)S(1)} %get-tuple-element.40) | copy-start | bytes 49156
  34.2 6.3 collective-permute-start
  46.5 16.1 %copy-start.32 = (f32[8192]{0:T(1024)S(1)}, f32[8192]{0:T(1024)}, u32[]{:S(2)}) copy-start(f32[8192]{0:T(1024)} %iota_convert_fusion) | copy-start | bytes 98308
  52.2 169.0 %all-to-all-start.2 = ((f32[1,4096,128]{2,0,1:T(1,128)}), f32[1,4096,128]{2,0,1:T(1,128)S(1)}, u32[]{:S(2)}, u32[]{:S(2)}) async-start(f32[1,4096,128]{2,0,1:T(1,128)} %copy.93), calls=%async_computation.2 | async-start | bytes 4194304 | tf_op jit(solution)/shard_map/all_to_all | solution.py:139
  221.2 40.8 %all-to-all-start = ((f32[1,4096,128]{2,0,1:T(1,128)}), f32[1,4096,128]{2,0,1:T(1,128)}, u32[]{:S(2)}, u32[]{:S(2)}) async-start(f32[1,4096,128]{2,0,1:T(1,128)} %copy.85), calls=%async_computation | async-start | bytes 4194304 | tf_op jit(solution)/shard_map/all_to_all | solution.py:138
  401.6 81.5 %all-to-all-start.3 = ((f32[64,1,8192]{2,1,0:T(1,128)}), f32[64,1,8192]{2,1,0:T(1,128)}, u32[]{:S(2)}, u32[]{:S(2)}) async-start(f32[64,1,8192]{2,1,0:T(1,128)} %reshape.405), calls=%async_computation.3 | async-start | bytes 4194304 | tf_op jit(solution)/shard_map/all_to_all | solution.py:145
  483.1 39.6 %all-to-all-start.1 = ((f32[64,1,8192]{2,1,0:T(1,128)}), f32[64,1,8192]{2,1,0:T(1,128)}, u32[]{:S(2)}, u32[]{:S(2)}) async-start(f32[64,1,8192]{2,1,0:T(1,128)} %reshape.403), calls=%async_computation.1 | async-start | bytes 4194304 | tf_op jit(solution)/shard_map/all_to_all | solution.py:144
  493.6 114.0 %reduce-scatter.2.cloned.1.call-start = ((), (), s32[]{:S(2)}) async-start(), calls=%async_computation.6 | async-start | bytes 12582912 | tf_op jit(solution)/shard_map/reduce_scatter | solution.py:174
  554.6 11.8 %copy-start.21 = (f32[1,1,4096]{2,1,0:T(1,128)S(1)}, f32[1,1,4096]{2,1,0:T(1,128)}, u32[]{:S(2)}) copy-start(f32[1,1,4096]{2,1,0:T(1,128)} %copy-done.20) | copy-start | bytes 49156
  554.6 11.8 %copy-start.23 = (f32[1,1,4096]{2,1,0:T(1,128)S(1)}, f32[1,1,4096]{2,1,0:T(1,128)}, u32[]{:S(2)}) copy-start(f32[1,1,4096]{2,1,0:T(1,128)} %copy-done.22) | copy-start | bytes 49156
  554.7 11.8 %copy-start.25 = (f32[1,1,4096]{2,1,0:T(1,128)S(1)}, f32[1,1,4096]{2,1,0:T(1,128)}, u32[]{:S(2)}) copy-start(f32[1,1,4096]{2,1,0:T(1,128)} %copy-done.24) | copy-start | bytes 49156
  566.5 9.9 %copy-start.14 = (f32[1,4096,128]{1,2,0:T(8,128)S(1)}, f32[1,4096,128]{1,2,0:T(8,128)}, u32[]{:S(2)}) copy-start(f32[1,4096,128]{1,2,0:T(8,128)} %get-tuple-element.15) | copy-start | bytes 6291460
  566.5 9.9 %copy-start.15 = (f32[1,4096,128]{1,2,0:T(8,128)S(1)}, f32[1,4096,128]{1,2,0:T(8,128)}, u32[]{:S(2)}) copy-start(f32[1,4096,128]{1,2,0:T(8,128)} %get-tuple-element.16) | copy-start | bytes 6291460
  570.1 6.3 collective-permute-start.1
  583.0 24.6 %copy-start.19 = (f32[1,4096,128]{1,2,0:T(8,128)S(1)}, f32[1,4096,128]{1,2,0:T(8,128)}, u32[]{:S(2)}) copy-start(f32[1,4096,128]{1,2,0:T(8,128)} %get-tuple-element.29) | copy-start | bytes 6291460
  583.0 170.5 %all-reduce.2.cloned.1.call-start = ((), (), s32[]{:S(2)}) async-start(), calls=%async_computation.7 | async-start | bytes 8388608 | tf_op jit(solution)/shard_map/psum | solution.py:175
  607.6 150.6 %copy-start.1 = (s32[4096,16]{0,1:T(8,128)S(1)}, s32[4096,16]{0,1:T(8,128)}, u32[]{:S(2)}) copy-start(s32[4096,16]{0,1:T(8,128)} %param.13) | copy-start | bytes 786436
  (20 other events, 151.5 us)
Sparse Core Ops, SparseCore 0:
  9.7 18.7 all-gather.1
  583.1 24.4 reduce-scatter.1
  613.4 140.0 all-reduce.1
where the time goes:
time: 772 us; the launch traced here: 765 us
  other arithmetic  249 us (32%)
  waiting for transfers between devices  191 us (25%)
  matrix products  170 us (22%)
  local copies, waits for them, and re-layouts  92 us (12%)
  starting transfers between devices  48.6 us (6%)
  between operations  14.7 us (2%)
    psum x1, waiting for transfers between devices, body(): embed_grad = lax.psum(half_grad, 'ctx')  144 us
    reduce_sum x1, other arithmetic, body(): jnp.sum(weight * jnp.exp(-decay_rate * positions.astype(jnp.float32)[None...  133 us
    unnamed x2, other arithmetic  76.8 us
    unnamed x79, local copies, waits for them, and re-layouts  34.9 us
    dot_general x3, matrix products, forward_dft(): jnp.einsum('bckt,tm->bckm', turned_imag, inner_sin, precision=HIGHEST)  30.9 us
    reduce_scatter x1, waiting for transfers between devices, body(): lax.psum_scatter(partial_grad, 'fsdp', scatter_dimension=1, tiled=True)  24.6 us
    dot_general x3, matrix products, forward_dft(): jnp.einsum('bckt,tm->bckm', turned_imag, inner_cos, precision=HIGHEST)  20.6 us
    all_to_all x3, local copies, waits for them, and re-layouts, body(): lax.all_to_all(conv_part, 'ctx', split_axis=2, concat_axis=1, tiled=True)  17.7 us
  transfers between devices with their start and end apart: 9, of which 4 were waited for; matrix products, arithmetic and copies ran while one was open for 39% of the time, Pallas kernels for 0%

commit v1 on v0

--- a/solution.py
+++ b/solution.py
@@ -172,7 +172,8 @@
     ).astype(jnp.float32)
     partial_grad = jnp.einsum("btv,bct->vc", one_hot, grad_signal, precision=HIGHEST)
     half_grad = lax.psum_scatter(partial_grad, "fsdp", scatter_dimension=1, tiled=True)
-    embed_grad = lax.psum(half_grad, "ctx")
+    parts = lax.all_gather(half_grad, "ctx", axis=0, tiled=False)
+    embed_grad = parts.sum(axis=0)
     return (mixer_local, embed_grad)
 
 

time: 772 us -> 1700 us (2.20)
  waiting for transfers between devices: 191 us -> 1040 us
  other arithmetic: 249 us -> 331 us
    all_gather x0 -> x1, waiting for transfers between devices: none -> 991 us  [body(): parts = lax.all_gather(half_grad, 'ctx', axis=0, tiled=False)]
    psum x1 -> x0, waiting for transfers between devices: 144 us -> none  [body(): embed_grad = lax.psum(half_grad, 'ctx')]
    reduce_sum x0 -> x1, other arithmetic: none -> 82.3 us  [body(): embed_grad = parts.sum(axis=0)]
    unnamed x79 -> x78, local copies, waits for them, and re-layouts: 34.9 us -> 30.2 us
  transfers between devices with their start and end apart: 9 -> 9, of which waited for: 4 -> 4; matrix products, arithmetic and copies ran while one was open for 39% -> 17% of each run, Pallas kernels for 0% -> 0%
where the time goes in v1:
time: 1700 us; the launch traced here: 1690 us
  waiting for transfers between devices  1040 us (61%)
  other arithmetic  331 us (19%)
  matrix products  170 us (10%)
  local copies, waits for them, and re-layouts  87.4 us (5%)
  starting transfers between devices  48.6 us (3%)
    all_gather x1, waiting for transfers between devices, body(): parts = lax.all_gather(half_grad, 'ctx', axis=0, tiled=False)  991 us
    reduce_sum x1, other arithmetic, body(): jnp.sum(weight * jnp.exp(-decay_rate * positions.astype(jnp.float32)[None...  133 us
    reduce_sum x1, other arithmetic, body(): embed_grad = parts.sum(axis=0)  82.3 us
    unnamed x2, other arithmetic  76.8 us
  transfers between devices with their start and end apart: 9, of which 4 were waited for; matrix products, arithmetic and copies ran while one was open for 17% of the time, Pallas kernels for 0%

profile of v1, /device:TPU:0, one launch (start us, length us, event | category | flops | bytes accessed | tf_op | source)
XLA Modules:
  0.0 1689.4 jit_solution(7698383766879408301)
XLA Ops:
  12.1 16.4 all-gather.4.cloned.1.call-done
  52.2 10.4 all-to-all-start.2
  62.6 133.4 %fusion.5 = f32[64,8192]{1,0:T(8,128)S(1)} fusion(s32[64,16]{1,0:T(8,128)S(1)} %copy.84, f32[8192]{0:T(1024)S(1)} %copy-done.32, f32[64,16]{1,0:T(8,128)S(1)} %copy.83, f32[64,16]{1,0:T(8,128)S(1)} %copy.82), kind=kLoop, calls=%fused_computation.9 | loop fusion | flops 150470656 | bytes 2142208 | tf_op jit(solution)/shard_map/reduce_sum | solution.py:127
  221.2 10.9 all-to-all-start
  232.2 8.8 fusion.58
  247.7 7.0 fusion.81
  254.7 7.3 fusion.83
  310.8 19.4 %multiply_add_fusion = (f32[64,128,128]{2,1,0:T(8,128)}, f32[64,128,128]{2,1,0:T(8,128)}, f32[64,128,128]{2,1,0:T(8,128)}, f32[64,128,128]{2,1,0:T(8,128)}) fusion(f32[64,128,128]{2,1,0:T(8,128)} %fusion.55, f32[64,128,128]{2,1,0:T(8,128)} %fusion.70, f32[64,128,128]{2,1,0:T(8,128)} %fusion.58, f32[64,128,128]{2,1,0:T(8,128)} %fusion.64, ...), kind=kOutput, calls=%fused_computation.63 | convolution fusion | flops 1629716480 | bytes 50462720 | tf_op jit(solution)/shard_map/bckt,tm->bckm/dot_general | solution.py:55
  330.1 6.5 fusion.147
  357.7 38.4 %reduce.2 = f32[8192,64]{1,0:T(8,128)} reduce(f32[8192,1,64]{2,1,0:T(1,128)} %bitcast.331, f32[]{:T(128)} %broadcast.309), dimensions={1}, to_apply=%bitcast.305.reduce_sub_computation | reduce | bytes 4194308
  401.6 10.7 all-to-all-start.3
  439.2 38.4 %reduce = f32[8192,64]{1,0:T(8,128)} reduce(f32[8192,1,64]{2,1,0:T(1,128)} %bitcast.332, f32[]{:T(128)} %broadcast.309), dimensions={1}, to_apply=%bitcast.303.reduce_sub_computation | reduce | bytes 4194308
  483.1 10.5 all-to-all-start.1
  494.0 7.5 reduce.3
  501.6 6.6 reshape.407
  508.1 9.1 copy.96
  522.7 7.5 reduce.1
  530.2 6.8 reshape.405
  536.9 10.5 copy.88
  554.7 10.9 multiply_add_fusion.3
  576.6 6.5 fusion.75
  583.1 24.6 %reduce-scatter.2.cloned.1.call-done = f32[512,2048]{1,0:T(8,128)} async-done(((f32[512,4096]{1,0:T(8,128)}), f32[512,2048]{1,0:T(8,128)}) %reduce-scatter.2.cloned.1.call-update) | async-done | bytes 4194320 | tf_op jit(solution)/shard_map/reduce_scatter | solution.py:174
  609.5 990.8 %all-gather.6.cloned.1.call-done = f32[32768,2048]{1,0:T(8,128)} async-done(((f32[512,2048]{1,0:T(8,128)}), f32[32768,2048]{1,0:T(8,128)}) %all-gather.6.cloned.1.call-update) | async-done | bytes 268435456 | tf_op jit(solution)/shard_map/all_gather | solution.py:175
  1600.3 82.3 %reduce_sum.19 = f32[512,2048]{1,0:T(8,128)} reduce(f32[64,512,2048]{2,1,0:T(8,128)} %bitcast.68, f32[]{:T(128)} %constant.81.clone.1), dimensions={0}, to_apply=%region_2.3 | reduce | flops 66060288 | bytes 272629760 | tf_op jit(solution)/shard_map/reduce_sum | solution.py:176
  (144 shorter events, 193.5 us)
Async XLA Ops:
  7.2 31.2 %copy-start = (s32[4096,16]{0,1:T(8,128)S(1)}, s32[4096,16]{0,1:T(8,128)}, u32[]{:S(2)}) copy-start(s32[4096,16]{0,1:T(8,128)} %param.13) | copy-start | bytes 786436
  7.2 21.3 %all-gather.4.cloned.1.call-start = ((), (), s32[]{:S(2)}) async-start(), calls=%async_computation.5 | async-start | bytes 6291456 | tf_op jit(solution)/shard_map/all_gather | solution.py:100
  12.0 29.7 %copy-start.20 = (f32[1,1,4096]{2,1,0:T(1,128)}, f32[1,1,4096]{2,1,0:T(1,128)S(1)}, u32[]{:S(2)}) copy-start(f32[1,1,4096]{2,1,0:T(1,128)S(1)} %get-tuple-element.36) | copy-start | bytes 49156
  12.0 29.7 %copy-start.22 = (f32[1,1,4096]{2,1,0:T(1,128)}, f32[1,1,4096]{2,1,0:T(1,128)S(1)}, u32[]{:S(2)}) copy-start(f32[1,1,4096]{2,1,0:T(1,128)S(1)} %get-tuple-element.38) | copy-start | bytes 49156
  12.0 29.7 %copy-start.24 = (f32[1,1,4096]{2,1,0:T(1,128)}, f32[1,1,4096]{2,1,0:T(1,128)S(1)}, u32[]{:S(2)}) copy-start(f32[1,1,4096]{2,1,0:T(1,128)S(1)} %get-tuple-element.41) | copy-start | bytes 49156
  12.0 29.7 %copy-start.26 = (f32[1,1,4096]{2,1,0:T(1,128)}, f32[1,1,4096]{2,1,0:T(1,128)S(1)}, u32[]{:S(2)}) copy-start(f32[1,1,4096]{2,1,0:T(1,128)S(1)} %get-tuple-element.34) | copy-start | bytes 49156
  12.0 29.7 %copy-start.28 = (f32[1,1,4096]{2,1,0:T(1,128)}, f32[1,1,4096]{2,1,0:T(1,128)S(1)}, u32[]{:S(2)}) copy-start(f32[1,1,4096]{2,1,0:T(1,128)S(1)} %get-tuple-element.35) | copy-start | bytes 49156
  12.0 29.7 %copy-start.30 = (f32[1,1,4096]{2,1,0:T(1,128)}, f32[1,1,4096]{2,1,0:T(1,128)S(1)}, u32[]{:S(2)}) copy-start(f32[1,1,4096]{2,1,0:T(1,128)S(1)} %get-tuple-element.40) | copy-start | bytes 49156
  34.2 6.3 collective-permute-start
  46.5 16.1 copy-start.32
  52.2 169.0 %all-to-all-start.2 = ((f32[1,4096,128]{2,0,1:T(1,128)}), f32[1,4096,128]{2,0,1:T(1,128)S(1)}, u32[]{:S(2)}, u32[]{:S(2)}) async-start(f32[1,4096,128]{2,0,1:T(1,128)} %copy.93), calls=%async_computation.2 | async-start | bytes 4194304 | tf_op jit(solution)/shard_map/all_to_all | solution.py:139
  221.2 40.8 %all-to-all-start = ((f32[1,4096,128]{2,0,1:T(1,128)}), f32[1,4096,128]{2,0,1:T(1,128)}, u32[]{:S(2)}, u32[]{:S(2)}) async-start(f32[1,4096,128]{2,0,1:T(1,128)} %copy.85), calls=%async_computation | async-start | bytes 4194304 | tf_op jit(solution)/shard_map/all_to_all | solution.py:138
  401.6 81.5 %all-to-all-start.3 = ((f32[64,1,8192]{2,1,0:T(1,128)}), f32[64,1,8192]{2,1,0:T(1,128)}, u32[]{:S(2)}, u32[]{:S(2)}) async-start(f32[64,1,8192]{2,1,0:T(1,128)} %reshape.406), calls=%async_computation.3 | async-start | bytes 4194304 | tf_op jit(solution)/shard_map/all_to_all | solution.py:145
  483.1 39.6 %all-to-all-start.1 = ((f32[64,1,8192]{2,1,0:T(1,128)}), f32[64,1,8192]{2,1,0:T(1,128)}, u32[]{:S(2)}, u32[]{:S(2)}) async-start(f32[64,1,8192]{2,1,0:T(1,128)} %reshape.404), calls=%async_computation.1 | async-start | bytes 4194304 | tf_op jit(solution)/shard_map/all_to_all | solution.py:144
  493.6 114.1 %reduce-scatter.2.cloned.1.call-start = ((), (), s32[]{:S(2)}) async-start(), calls=%async_computation.6 | async-start | bytes 12582912 | tf_op jit(solution)/shard_map/reduce_scatter | solution.py:174
  554.6 11.9 copy-start.21
  554.6 11.9 copy-start.23
  554.7 11.9 copy-start.25
  566.6 9.9 copy-start.14
  566.6 9.9 copy-start.15
  570.2 6.3 collective-permute-start.1
  583.1 24.6 %copy-start.19 = (f32[1,4096,128]{1,2,0:T(8,128)S(1)}, f32[1,4096,128]{1,2,0:T(8,128)}, u32[]{:S(2)}) copy-start(f32[1,4096,128]{1,2,0:T(8,128)} %get-tuple-element.29) | copy-start | bytes 6291460
  583.1 1017.3 %all-gather.6.cloned.1.call-start = ((), (), s32[]{:S(2)}) async-start(), calls=%async_computation.7 | async-start | bytes 272629760 | tf_op jit(solution)/shard_map/all_gather | solution.py:175
  1600.3 82.3 %copy-start.1 = (s32[4096,16]{0,1:T(8,128)S(1)}, s32[4096,16]{0,1:T(8,128)}, u32[]{:S(2)}) copy-start(s32[4096,16]{0,1:T(8,128)} %param.13) | copy-start | bytes 786436
  (20 other events, 151.5 us)
Sparse Core Ops, SparseCore 0:
  9.7 18.7 all-gather.3
  583.2 24.4 reduce-scatter.1
  611.0 989.3 all-gather.5
